TPU v7x, 32 devices: a whole 2x2x4 slice. The times are simulated.
32 devices in a mesh: seq: 8 (over y, x, core), head: 4 (over z).
Axes of the slice: x: 2, y: 2, z: 4, core: 2. Of those that a mesh axis runs over, the one named last changes fastest.
Arguments:
- out_grad: bfloat16 [2048, 4096], P('seq', 'head'), may hold values from -7.2 to 7.2
- x_in: bfloat16 [2048, 4096], P('seq', 'head'), may hold values from -6 to 6
- b_in: bfloat16 [2048, 128], P('seq'), may hold values from -2.5 to 2.5
- c_in: bfloat16 [2048, 128], P('seq'), may hold values from -2.5 to 2.5
- dt_raw: float32 [64, 2048], P('head', 'seq'), may hold values from -5.1 to -0.7
- dt_bias: float32 [64], P('head'), may hold values from -0.5 to 0.5
- a_log: float32 [64], P('head'), may hold values from -7.5 to 2.2
- d_skip: float32 [64], P('head'), may hold values from 0.5 to 1.5
- states: bfloat16 [8, 4096, 128], P('seq', 'head'), may hold values from -6 to 6
- w_out: bfloat16 [4096, 4096], P('head'), may hold values from -0.09375 to 0.09375
- w_in: bfloat16 [4096, 4096], P(None, 'head'), may hold values from -0.125 to 0.125
Outputs:
- in_grad: bfloat16 [4096, 2048], P('head', 'seq')
- bc_grad: bfloat16 [256, 2048], P('head', 'seq')
- dt_grad: float32 [64, 2048], P('head', 'seq')
- param_grad: float32 [3, 64], P(None, 'head')
All inputs are finite; a program needn't handle non-finite values.
Results may differ from a plain program's by a relative error of at most 0.015.
Values may be sent and summed in bfloat16 or wider, within the bound.
A program may use at most 64 MiB of HBM per device.

v0:
```python
import jax
import jax.numpy as jnp
from jax import lax
from jax.sharding import PartitionSpec as P


def partners(count, distance):
    return [(place, place ^ distance) for place in range(count)]


def entering(decay, state, axis):
    count, mine = (lax.axis_size(axis), lax.axis_index(axis))
    carried = jnp.zeros_like(state)
    reach = jnp.ones_like(decay)
    distance = 1
    while distance < count:
        pairs = partners(count, distance)
        other_decay = lax.ppermute(decay, axis, pairs)
        other_state = lax.ppermute(state.astype(jnp.bfloat16), axis, pairs).astype(jnp.float32)
        earlier = mine // distance % 2 == 0
        carried = jnp.where(earlier, carried + reach[:, None, None] * other_state, carried)
        reach = jnp.where(earlier, reach * other_decay, reach)
        state = jnp.where(
            earlier,
            state + decay[:, None, None] * other_state,
            other_state + other_decay[:, None, None] * state,
        )
        decay = decay * other_decay
        distance *= 2
    return carried


def summed(value, axis):
    count = lax.axis_size(axis)
    distance = 1
    while distance < count:
        value = value + lax.ppermute(value, axis, partners(count, distance))
        distance *= 2
    return value


def shards(out_grad, x_in, b_in, c_in, dt_raw, dt_bias, a_log, d_skip, states, w_out, w_in):
    tokens_here, inner_here = x_in.shape
    group_heads = dt_raw.shape[0]
    head_dim = inner_here // group_heads
    state_dim = b_in.shape[1]
    contract_last = (((1,), (1,)), ((), ()))
    head_sum = lax.dot_general(
        lax.all_gather(out_grad, "head", axis=1, tiled=True),
        w_out,
        contract_last,
        preferred_element_type=jnp.float32,
    )
    dy_heads = head_sum.astype(jnp.bfloat16).reshape(tokens_here, group_heads, head_dim)
    dy_wide = dy_heads.astype(jnp.float32)
    x_heads = x_in.reshape(tokens_here, group_heads, head_dim)
    x_wide = x_heads.astype(jnp.float32)
    decay_rate = jnp.exp(a_log)
    step_size = jax.nn.softplus(dt_raw + dt_bias[:, None])
    log_step = -decay_rate[:, None] * step_size
    cumlog = jnp.cumsum(log_step, axis=1)
    positions = jnp.arange(tokens_here)
    causal = positions[:, None] >= positions[None, :]
    log_gaps = cumlog[:, :, None] - cumlog[:, None, :]
    decay_mask = jnp.where(causal[None], jnp.exp(jnp.minimum(log_gaps, 0.0)), 0.0)
    scores = lax.dot_general(c_in, b_in, contract_last, preferred_element_type=jnp.float32)
    step_rows = step_size.T
    x_scaled = (x_wide * step_rows[:, :, None]).astype(jnp.bfloat16)
    pair_dots = jnp.einsum("ihp,jhp->hij", dy_heads, x_scaled, preferred_element_type=jnp.float32)
    kernel = (scores[None] * decay_mask).astype(jnp.bfloat16)
    intra_back = jnp.einsum("hij,ihp->jhp", kernel, dy_heads, preferred_element_type=jnp.float32)
    masked_dots = (pair_dots * decay_mask).astype(jnp.bfloat16)
    start_decay = jnp.exp(cumlog)
    dy_decay = (dy_wide * start_decay.T[:, :, None]).astype(jnp.bfloat16)
    local_state = jnp.einsum("ihp,in->hpn", dy_decay, c_in, preferred_element_type=jnp.float32)
    end_total = jnp.exp(cumlog[:, -1])
    entry_state = states.reshape(group_heads, head_dim, state_dim)
    db_intra = jnp.einsum("hij,in->nj", masked_dots, c_in, preferred_element_type=jnp.float32)
    dc_intra = jnp.einsum("hij,jn->ni", masked_dots, b_in, preferred_element_type=jnp.float32)
    dc_entry = jnp.einsum("ihp,hpn->ni", dy_decay, entry_state, preferred_element_type=jnp.float32)
    ystate = jnp.einsum("in,hpn->ihp", c_in, entry_state, preferred_element_type=jnp.float32)
    pair_weight = pair_dots * scores[None] * decay_mask
    state_terms = start_decay * jnp.sum(dy_wide * ystate, axis=2).T
    skip_terms = jnp.sum(dy_wide * x_wide, axis=(0, 2))
    carried = entering(end_total, local_state, "seq")
    carried_bf = carried.astype(jnp.bfloat16)
    state_back = jnp.einsum("jn,hpn->jhp", b_in, carried_bf, preferred_element_type=jnp.float32)
    end_decay = jnp.exp(cumlog[:, -1:] - cumlog)
    end_weight = (step_size * end_decay).T
    x_grad = (
        (
            step_rows[:, :, None] * intra_back
            + end_weight[:, :, None] * state_back
            + d_skip[None, :, None] * dy_wide
        )
        .astype(jnp.bfloat16)
        .reshape(tokens_here, inner_here)
    )
    x_end = (x_wide * end_weight[:, :, None]).astype(jnp.bfloat16)
    db_entry = jnp.einsum("jhp,hpn->nj", x_end, carried_bf, preferred_element_type=jnp.float32)
    bc_part = jnp.concatenate([db_intra + db_entry, dc_intra + dc_entry], axis=0)
    end_terms = end_weight.T * jnp.sum(x_wide * state_back, axis=2).T
    cum_grad = pair_weight.sum(axis=2) - pair_weight.sum(axis=1) + state_terms - end_terms
    tail_grad = end_terms.sum(axis=1) + end_total * jnp.sum(
        entry_state.astype(jnp.float32) * carried, axis=(1, 2)
    )
    cum_grad = cum_grad.at[:, -1].add(tail_grad)
    step_grad = jnp.cumsum(cum_grad[:, ::-1], axis=1)[:, ::-1]
    dt_sum = (
        -decay_rate[:, None] * step_grad
        + jnp.sum(x_wide * (intra_back + end_decay.T[:, :, None] * state_back), axis=2).T
    )
    dt_grad = dt_sum * jax.nn.sigmoid(dt_raw + dt_bias[:, None])
    param_terms = jnp.stack(
        [jnp.sum(step_grad * log_step, axis=1), skip_terms, jnp.sum(dt_grad, axis=1)]
    )
    heads_count = lax.axis_size("head")
    in_term = lax.dot_general(
        w_in, x_grad, contract_last, preferred_element_type=jnp.float32
    ).astype(jnp.bfloat16)
    rows_here = in_term.shape[0] // heads_count
    both = jnp.concatenate(
        [
            in_term.reshape(heads_count, rows_here, tokens_here),
            bc_part.astype(jnp.bfloat16).reshape(heads_count, -1, tokens_here),
        ],
        axis=1,
    )
    both_sum = lax.psum_scatter(
        both.reshape(-1, tokens_here), "head", scatter_dimension=0, tiled=True
    )
    in_part, bc_sum = (both_sum[:rows_here], both_sum[rows_here:])
    norm_scale = (lax.axis_size("seq") * tokens_here * head_dim) ** (-0.5)
    param_grad = summed(param_terms, "seq") * norm_scale
    return (in_part, bc_sum, dt_grad, param_grad)


def solution(mesh):
    return jax.shard_map(
        shards,
        mesh=mesh,
        in_specs=(
            P("seq", "head"),
            P("seq", "head"),
            P("seq", None),
            P("seq", None),
            P("head", "seq"),
            P("head"),
            P("head"),
            P("head"),
            P("seq", "head", None),
            P("head", None),
            P(None, "head"),
        ),
        out_specs=(P("head", "seq"), P("head", "seq"), P("head", "seq"), P(None, "head")),
        check_vma=False,
    )
```

profile of v0, /device:TPU:0, one launch (start us, length us, event | category | flops | bytes accessed | tf_op | source)
XLA Modules:
  0.0 161.3 jit_solution(2156898000324561240)
XLA Ops:
  7.2 0.7 all-gather.2.cloned.1.call-update
  8.0 0.8 copy.92
  8.8 0.7 exponential_negate_fusion
  9.5 0.7 broadcast_multiply_fusion
  10.3 0.6 reduce-window.14
  11.3 0.6 collective-permute-start.1
  11.8 0.8 fusion.36
  12.6 0.7 copy.114
  13.3 0.7 copy.99
  13.9 0.7 copy.93
  14.7 0.7 iota_compare_fusion
  15.3 1.0 fusion.53
  16.4 1.3 copy.102
  17.8 3.0 %collective-permute-start.3 = (f32[16]{0:T(128)S(1)}, f32[16]{0:T(128)S(1)}, u32[]{:S(2)}, u32[]{:S(2)}) collective-permute-start(f32[16]{0:T(128)S(1)} %fusion.46), channel_id=1, source_target_pairs={{0,8},{4,12},{8,0},{12,4},{16,24},{20,28},{24,16},{28,20},{1,9},{5... | collective-permute-start | bytes 200 | tf_op jit(solution)/shard_map/ppermute | solution.py:18
  20.8 1.3 copy.103
  22.3 0.6 copy-done.23
  22.9 0.6 broadcast_select_fusion
  23.5 34.5 %all-gather.2.cloned.1.call-done = bf16[256,4096]{1,0:T(8,128)(2,1)} async-done(((bf16[256,1024]{1,0:T(8,128)(2,1)}), bf16[256,4096]{1,0:T(8,128)(2,1)}) %all-gather.2.cloned.1.call-update) | async-done | bytes 2097168 | tf_op jit(solution)/shard_map/all_gather | solution.py:49
  58.0 7.2 %fusion.16 = (f32[1024]{0:T(1024)}, bf16[256,1024]{1,0:T(8,128)(2,1)S(1)}, bf16[256,1024]{1,0:T(8,128)(2,1)S(1)}) fusion(bf16[256,1024]{1,0:T(8,128)(2,1)S(1)} %copy-done.4, f32[256,1024]{1,0:T(8,128)} %copy.103, bf16[256,4096]{1,0:T(8,128)(2,1)} %all-gather.2.cloned.1.call-done, bf16[1024,4096]{1,0:T(8,128)(2,1)} %param.22), kind=kOutput, calls=%fused_computation.34 | convolution fusion | flops 2149317632 | bytes 13111296 | tf_op jit(solution)/shard_map/dot_general | solution.py:48
  66.1 4.0 %fusion.1 = (f32[16,256]{1,0:T(8,128)}, f32[16,256]{1,0:T(8,128)}, bf16[256,256]{1,0:T(8,128)(2,1)S(1)}) fusion(f32[16,256]{1,0:T(8,128)} %copy-done.7, f32[256,256]{1,0:T(8,128)S(1)} %fusion.53, pred[256,256]{1,0:T(8,128)(4,1)} %iota_compare_fusion, bf16[256,16,64]{0,2,1:T(8,128)(2,1)S(1)} %bitcast.112, f32[256,16,64]{0,2,1:T(8,128)S(1)} %bitcast.118, ...), kind=kOutput, calls=%fused_computation.7 | convolution fusion | flops 146202624 | bytes 2097152 | tf_op jit(solution)/shard_map/ihp,jhp->hij/dot_general | solution.py:69
  70.3 1.5 collective-permute-start.2
  71.9 3.2 %fusion.9 = f32[256,16,64]{0,2,1:T(8,128)} fusion(bf16[256,16,64]{0,2,1:T(8,128)(2,1)S(1)} %bitcast.113, f32[16,256]{1,0:T(8,128)S(1)} %copy-done.8, f32[256,256]{1,0:T(8,128)} %copy-done.6, pred[256,256]{1,0:T(8,128)(4,1)S(1)} %copy-done.9), kind=kOutput, calls=%fused_computation.19 | convolution fusion | flops 139460608 | bytes 1916928 | tf_op jit(solution)/shard_map/hij,ihp->jhp/dot_general | solution.py:71
  75.1 4.0 %collective-permute-done.2 = bf16[16,64,128]{2,1,0:T(8,128)(2,1)S(1)} collective-permute-done((bf16[16,64,128]{2,1,0:T(8,128)(2,1)S(1)}, bf16[16,64,128]{2,1,0:T(8,128)(2,1)S(1)}, u32[]{:S(2)}, u32[]{:S(2)}) %collective-permute-start.2) | collective-permute-done | bytes 262176 | tf_op jit(solution)/shard_map/ppermute | solution.py:19
  79.4 1.5 collective-permute-start.4
  81.5 5.9 %collective-permute-done.4 = bf16[16,64,128]{2,1,0:T(8,128)(2,1)S(1)} collective-permute-done((bf16[16,64,128]{2,1,0:T(8,128)(2,1)S(1)}, bf16[16,64,128]{2,1,0:T(8,128)(2,1)S(1)}, u32[]{:S(2)}, u32[]{:S(2)}) %collective-permute-start.4) | collective-permute-done | bytes 262176 | tf_op jit(solution)/shard_map/ppermute | solution.py:19
  87.4 0.4 convolution_bitcast_fusion.2
  88.1 0.9 copy.105
  88.9 2.6 %multiply_reduce_fusion.1 = (f32[256,16]{0,1:T(8,128)}, f32[256,16]{0,1:T(8,128)}, bf16[256,16,64]{0,2,1:T(8,128)(2,1)S(1)}) fusion(f32[256,1024]{0,1:T(8,128)S(1)} %copy.102, f32[256,16,64]{0,2,1:T(8,128)} %fusion.9, f32[256,16]{0,1:T(8,128)S(1)} %copy-done.10, bf16[256,1024]{0,1:T(8,128)(2,1)S(1)} %copy.94, f32[16]{0:T(128)} %param.20, ...), kind=kOutput, calls=%fused_computation.39 | convolution fusion | flops 71950336 | bytes 4079811 | tf_op jit(solution)/shard_map/jn,hpn->jhp/dot_general | solution.py:87
  91.6 5.8 %fusion = bf16[4096,256]{0,1:T(8,128)(2,1)S(1)} fusion(bf16[256,1024]{0,1:T(8,128)(2,1)S(1)} %bitcast.133, bf16[4096,1024]{1,0:T(8,128)(2,1)} %param.23), kind=kOutput, calls=%fused_computation.1 | convolution fusion | flops 2148532224 | bytes 11010048 | tf_op jit(solution)/shard_map/dot_general | solution.py:118
  97.4 2.8 %reshape.138 = bf16[4,1024,256]{1,0,2:T(4,128)(2,1)} reshape(bf16[4096,256]{0,1:T(8,128)(2,1)S(1)} %fusion) | data formatting | bytes 4194304 | tf_op jit(solution)/shard_map/reshape | solution.py:124
  100.2 2.8 %pad_maximum_fusion = bf16[4,1088,256]{1,0,2:T(4,128)(2,1)S(1)} fusion(bf16[4,64,256]{1,0,2:T(4,128)(2,1)} %copy.105, bf16[4,1024,256]{1,0,2:T(4,128)(2,1)} %reshape.138), kind=kLoop, calls=%fused_computation.9 | loop fusion | flops 4456448 | bytes 4456448 | tf_op jit(solution)/shard_map/concatenate | solution.py:122
  103.0 3.6 %copy.106 = bf16[4,1088,256]{2,1,0:T(8,128)(2,1)} copy(bf16[4,1088,256]{1,0,2:T(4,128)(2,1)S(1)} %pad_maximum_fusion) | data formatting | bytes 4456448 | tf_op jit(solution)/shard_map/concatenate | solution.py:122
  106.6 0.7 reduce_sum.126
  107.5 1.3 fusion.10
  108.8 0.8 copy.108
  109.7 0.8 copy.110
  110.6 1.6 %multiply_reduce_fusion.2 = f32[16]{0:T(128)S(1)} fusion(bf16[16,64,128]{2,1,0:T(8,128)(2,1)} %bitcast.116, bf16[16,64,128]{2,1,0:T(8,128)(2,1)} %copy-done.5, f32[16]{0:T(128)} %get-tuple-element.35, bf16[16,64,128]{2,1,0:T(8,128)(2,1)} %copy-done.2, f32[16]{0:T(128)} %get-tuple-element.36, bf16[16,64,128]{2,1,0:T(8,128)(2,1)S(1)} %collective-permute-done, ...), kind=kLoop, calls=%fused_computation.57 | loop fusion | flops 1703920 | bytes 1048771 | tf_op jit(solution)/shard_map/reduce_sum | solution.py:104
  112.5 0.6 reduce-window.16
  114.0 1.1 collective-permute-done.5
  115.1 1.4 collective-permute-start.6
  116.5 2.2 %collective-permute-done.6 = f32[3,16]{1,0:T(4,128)S(1)} collective-permute-done((f32[3,16]{1,0:T(4,128)S(1)}, f32[3,16]{1,0:T(4,128)S(1)}, u32[]{:S(2)}, u32[]{:S(2)}) %collective-permute-start.6) | collective-permute-done | bytes 224 | tf_op jit(solution)/shard_map/ppermute | solution.py:37
  118.8 1.4 collective-permute-start.7
  120.2 0.7 copy.116
  120.9 1.6 collective-permute-done.7
  122.4 0.6 add_multiply_fusion
  123.0 28.2 %reduce-scatter.2.cloned.1.call-done = bf16[1088,256]{1,0:T(8,128)(2,1)} async-done(((bf16[4352,256]{1,0:T(8,128)(2,1)}), bf16[1088,256]{1,0:T(8,128)(2,1)}) %reduce-scatter.2.cloned.1.call-update) | async-done | bytes 557072 | tf_op jit(solution)/shard_map/reduce_scatter | solution.py:129
  151.2 1.4 slice.50
  152.6 1.9 %slice.49 = bf16[1024,256]{1,0:T(8,128)(2,1)} slice(bf16[1088,256]{1,0:T(8,128)(2,1)} %reduce-scatter.2.cloned.1.call-done), slice={[0:1024], [0:256]} | slice | bytes 1048576 | tf_op jit(solution)/shard_map/slice | solution.py:132
  (104 shorter events, 4.5 us)
Async XLA Ops:
  7.2 8.2 %copy-start = (bf16[256,128]{1,0:T(8,128)(2,1)S(1)}, bf16[256,128]{1,0:T(8,128)(2,1)}, u32[]{:S(2)}) copy-start(bf16[256,128]{1,0:T(8,128)(2,1)} %param.15) | copy-start | bytes 196612
  7.2 50.8 %copy-start.4 = (bf16[256,1024]{1,0:T(8,128)(2,1)S(1)}, bf16[256,1024]{1,0:T(8,128)(2,1)}, u32[]{:S(2)}) copy-start(bf16[256,1024]{1,0:T(8,128)(2,1)} %param.14) | copy-start | bytes 1572868
  7.2 50.8 %all-gather.2.cloned.1.call-start = ((), (), s32[]{:S(2)}) async-start(), calls=%async_computation.1 | async-start | bytes 2621440 | tf_op jit(solution)/shard_map/all_gather | solution.py:49
  7.9 143.3 %reduce-scatter.2.cloned.1.call-start = ((), (), s32[]{:S(2)}) async-start(), calls=%async_computation.2 | async-start | bytes 2785280 | tf_op jit(solution)/shard_map/reduce_scatter | solution.py:129
  9.5 0.8 copy-start.25
  11.1 0.7 copy-start.7
  11.3 11.0 %copy-start.19 = (f32[16]{0:T(128)}, f32[16]{0:T(128)S(1)}, u32[]{:S(2)}) copy-start(f32[16]{0:T(128)S(1)} %fusion.45) | copy-start | bytes 196
  11.3 6.5 %collective-permute-start.1 = (f32[16]{0:T(128)S(1)}, f32[16]{0:T(128)S(1)}, u32[]{:S(2)}, u32[]{:S(2)}) collective-permute-start(f32[16]{0:T(128)S(1)} %fusion.45), channel_id=1, source_target_pairs={{0,4},{4,0},{8,12},{12,8},{16,20},{20,16},{24,28},{28,24},{1,5},{5... | collective-permute-start | bytes 200 | tf_op jit(solution)/shard_map/ppermute | solution.py:18
  11.8 3.5 %copy-start.21 = (f32[16]{0:T(128)}, f32[16]{0:T(128)S(1)}, u32[]{:S(2)}) copy-start(f32[16]{0:T(128)S(1)} %slice_bitcast_fusion) | copy-start | bytes 196
  16.4 49.7 %copy-start.6 = (f32[256,256]{1,0:T(8,128)}, f32[256,256]{1,0:T(8,128)S(1)}, u32[]{:S(2)}) copy-start(f32[256,256]{1,0:T(8,128)S(1)} %fusion.53) | copy-start | bytes 786436
  17.7 4.5 %copy-start.15 = (f32[16]{0:T(128)}, f32[16]{0:T(128)S(1)}, u32[]{:S(2)}) copy-start(f32[16]{0:T(128)S(1)} %collective-permute-done.1) | copy-start | bytes 196
  17.8 4.5 %copy-start.27 = (f32[16]{0:T(128)}, f32[16]{0:T(128)S(1)}, u32[]{:S(2)}) copy-start(f32[16]{0:T(128)S(1)} %fusion.46) | copy-start | bytes 196
  17.8 4.5 %collective-permute-start.3 = (f32[16]{0:T(128)S(1)}, f32[16]{0:T(128)S(1)}, u32[]{:S(2)}, u32[]{:S(2)}) collective-permute-start(f32[16]{0:T(128)S(1)} %fusion.46), channel_id=1, source_target_pairs={{0,8},{4,12},{8,0},{12,4},{16,24},{20,28},{24,16},{28,20},{1,9},{5... | collective-permute-start | bytes 200 | tf_op jit(solution)/shard_map/ppermute | solution.py:18
  22.3 0.6 copy-start.23
  23.5 42.2 %copy-start.3 = (bf16[256,128]{1,0:T(8,128)(2,1)S(1)}, bf16[256,128]{1,0:T(8,128)(2,1)}, u32[]{:S(2)}) copy-start(bf16[256,128]{1,0:T(8,128)(2,1)} %param.16) | copy-start | bytes 196612
  65.9 4.1 %collective-permute-start = (bf16[16,64,128]{2,1,0:T(8,128)(2,1)S(1)}, bf16[16,64,128]{2,1,0:T(8,128)(2,1)S(1)}, u32[]{:S(2)}, u32[]{:S(2)}) collective-permute-start(bf16[16,64,128]{2,1,0:T(8,128)(2,1)S(1)} %get-tuple-element.48), channel_id=1, source_target_pairs={{0,4},{4,0},{8,12},{12,8},{16,20},{20,16},{24,28},{28,24},{1,5},{5... | collective-permute-start | bytes 786440 | tf_op jit(solution)/shard_map/ppermute | solution.py:19
  66.0 4.1 %copy-start.16 = (f32[16]{0:T(128)S(1)}, f32[16]{0:T(128)}, u32[]{:S(2)}) copy-start(f32[16]{0:T(128)} %copy-done.15) | copy-start | bytes 196
  66.0 4.0 %copy-start.20 = (f32[16]{0:T(128)S(1)}, f32[16]{0:T(128)}, u32[]{:S(2)}) copy-start(f32[16]{0:T(128)} %copy-done.19) | copy-start | bytes 196
  66.0 5.8 %copy-start.8 = (f32[16,256]{1,0:T(8,128)S(1)}, f32[16,256]{1,0:T(8,128)}, u32[]{:S(2)}) copy-start(f32[16,256]{1,0:T(8,128)} %copy-done.7) | copy-start | bytes 49156
  66.1 5.8 %copy-start.9 = (pred[256,256]{1,0:T(8,128)(4,1)S(1)}, pred[256,256]{1,0:T(8,128)(4,1)}, u32[]{:S(2)}) copy-start(pred[256,256]{1,0:T(8,128)(4,1)} %iota_compare_fusion) | copy-start | bytes 196612
  70.1 9.0 %copy-start.24 = (f32[16]{0:T(128)S(1)}, f32[16]{0:T(128)}, u32[]{:S(2)}) copy-start(f32[16]{0:T(128)} %copy-done.23) | copy-start | bytes 196
  70.1 9.0 %copy-start.28 = (f32[16]{0:T(128)S(1)}, f32[16]{0:T(128)}, u32[]{:S(2)}) copy-start(f32[16]{0:T(128)} %copy-done.27) | copy-start | bytes 196
  70.3 10.7 %copy-start.1 = (bf16[1,1024,128]{2,1,0:T(8,128)(2,1)S(1)}, bf16[1,1024,128]{2,1,0:T(8,128)(2,1)}, u32[]{:S(2)}) copy-start(bf16[1,1024,128]{2,1,0:T(8,128)(2,1)} %param.21) | copy-start | bytes 786436
  70.3 17.0 %copy-start.11 = (f32[256,16]{0,1:T(8,128)S(1)}, f32[256,16]{0,1:T(8,128)}, u32[]{:S(2)}) copy-start(f32[256,16]{0,1:T(8,128)} %copy.99) | copy-start | bytes 49156
  70.3 17.0 %copy-start.17 = (f32[16]{0:T(128)S(1)}, f32[16]{0:T(128)}, u32[]{:S(2)}) copy-start(f32[16]{0:T(128)} %get-tuple-element.35) | copy-start | bytes 196
  70.3 17.0 %copy-start.18 = (f32[16]{0:T(128)S(1)}, f32[16]{0:T(128)}, u32[]{:S(2)}) copy-start(f32[16]{0:T(128)} %get-tuple-element.36) | copy-start | bytes 196
  70.3 8.8 %collective-permute-start.2 = (bf16[16,64,128]{2,1,0:T(8,128)(2,1)S(1)}, bf16[16,64,128]{2,1,0:T(8,128)(2,1)S(1)}, u32[]{:S(2)}, u32[]{:S(2)}) collective-permute-start(bf16[16,64,128]{2,1,0:T(8,128)(2,1)S(1)} %fusion.48), channel_id=1, source_target_pairs={{0,8},{4,12},{8,0},{12,4},{16,24},{20,28},{24,16},{28,20},{1,9},{5... | collective-permute-start | bytes 786440 | tf_op jit(solution)/shard_map/ppermute | solution.py:19
  75.1 13.8 %copy-start.10 = (f32[256,16]{0,1:T(8,128)S(1)}, f32[256,16]{0,1:T(8,128)}, u32[]{:S(2)}) copy-start(f32[256,16]{0,1:T(8,128)} %copy.114) | copy-start | bytes 49156
  79.1 12.4 %copy-start.2 = (bf16[16,64,128]{2,1,0:T(8,128)(2,1)}, bf16[16,64,128]{2,1,0:T(8,128)(2,1)S(1)}, u32[]{:S(2)}) copy-start(bf16[16,64,128]{2,1,0:T(8,128)(2,1)S(1)} %collective-permute-done.2) | copy-start | bytes 786436
  79.4 7.9 %collective-permute-start.4 = (bf16[16,64,128]{2,1,0:T(8,128)(2,1)S(1)}, bf16[16,64,128]{2,1,0:T(8,128)(2,1)S(1)}, u32[]{:S(2)}, u32[]{:S(2)}) collective-permute-start(bf16[16,64,128]{2,1,0:T(8,128)(2,1)S(1)} %fusion.24), channel_id=1, source_target_pairs={{0,16},{4,20},{8,24},{12,28},{16,0},{20,4},{24,8},{28,12},{1,17},{... | collective-permute-start | bytes 786440 | tf_op jit(solution)/shard_map/ppermute | solution.py:19
  87.3 10.0 %copy-start.5 = (bf16[16,64,128]{2,1,0:T(8,128)(2,1)}, bf16[16,64,128]{2,1,0:T(8,128)(2,1)S(1)}, u32[]{:S(2)}) copy-start(bf16[16,64,128]{2,1,0:T(8,128)(2,1)S(1)} %collective-permute-done.4) | copy-start | bytes 786436
  103.0 6.6 %copy-start.13 = (f32[16,256]{1,0:T(8,128)S(1)}, f32[16,256]{1,0:T(8,128)}, u32[]{:S(2)}) copy-start(f32[16,256]{1,0:T(8,128)} %get-tuple-element.29) | copy-start | bytes 49156
  106.6 5.6 %copy-start.14 = (f32[16]{0:T(128)S(1)}, f32[16]{0:T(128)}, u32[]{:S(2)}) copy-start(f32[16]{0:T(128)} %param.18) | copy-start | bytes 196
  106.6 5.6 %copy-start.22 = (f32[16]{0:T(128)S(1)}, f32[16]{0:T(128)}, u32[]{:S(2)}) copy-start(f32[16]{0:T(128)} %copy-done.21) | copy-start | bytes 196
  106.6 7.0 %copy-start.12 = (f32[256,16]{0,1:T(8,128)S(1)}, f32[256,16]{0,1:T(8,128)}, u32[]{:S(2)}) copy-start(f32[256,16]{0,1:T(8,128)} %get-tuple-element.32) | copy-start | bytes 49156
  106.6 7.2 %copy-start.26 = (f32[16]{0:T(128)S(1)}, f32[16]{0:T(128)}, u32[]{:S(2)}) copy-start(f32[16]{0:T(128)} %copy-done.25) | copy-start | bytes 196
  113.9 1.2 collective-permute-start.5
  115.1 3.7 %collective-permute-start.6 = (f32[3,16]{1,0:T(4,128)S(1)}, f32[3,16]{1,0:T(4,128)S(1)}, u32[]{:S(2)}, u32[]{:S(2)}) collective-permute-start(f32[3,16]{1,0:T(4,128)S(1)} %fusion.47), channel_id=1, source_target_pairs={{0,8},{4,12},{8,0},{12,4},{16,24},{20,28},{24,16},{28,20},{1,9},{5... | collective-permute-start | bytes 584 | tf_op jit(solution)/shard_map/ppermute | solution.py:37
  118.8 3.7 %collective-permute-start.7 = (f32[3,16]{1,0:T(4,128)S(1)}, f32[3,16]{1,0:T(4,128)S(1)}, u32[]{:S(2)}, u32[]{:S(2)}) collective-permute-start(f32[3,16]{1,0:T(4,128)S(1)} %fusion.69), channel_id=1, source_target_pairs={{0,16},{4,20},{8,24},{12,28},{16,0},{20,4},{24,8},{28,12},{1,17},{... | collective-permute-start | bytes 584 | tf_op jit(solution)/shard_map/ppermute | solution.py:37
Sparse Core Ops, SparseCore 0:
  9.6 48.3 all-gather.1
  106.7 44.4 reduce-scatter.1
where the time goes:
time: 162 us; the launch traced here: 161 us
  waiting for transfers between devices  78.4 us (48%)
  matrix products  26.6 us (16%)
  local copies, waits for them, and re-layouts  21.4 us (13%)
  between operations  14.4 us (9%)
  other arithmetic  10.9 us (7%)
  starting transfers between devices  9.59 us (6%)
    all_gather x1, waiting for transfers between devices, shards(): lax.all_gather(out_grad, 'head', axis=1, tiled=True)  34.5 us
    reduce_scatter x1, waiting for transfers between devices, shards(): lax.psum_scatter(both.reshape(-1, tokens_here), 'head', scatter_dimension...  28.2 us
    ppermute x3, waiting for transfers between devices, entering(): lax.ppermute(state.astype(jnp.bfloat16), axis, pairs).astype(jnp.float32)  9.91 us
    dot_general x1, matrix products, shards(): lax.dot_general(lax.all_gather(out_grad, 'head', axis=1, tiled=True), w_o...  7.21 us
    dot_general x1, matrix products, shards(): lax.dot_general(w_in, x_grad, contract_last, preferred_element_type=jnp.f...  5.8 us
    ppermute x3, waiting for transfers between devices, summed(): value = value + lax.ppermute(value, axis, partners(count, distance))  4.97 us
    dot_general x1, matrix products, shards(): jnp.einsum('ihp,jhp->hij', dy_heads, x_scaled, preferred_element_type=jnp...  4 us
    concatenate x1, local copies, waits for them, and re-layouts, shards(): jnp.concatenate([in_term.reshape(heads_count, rows_here, tokens_here), bc...  3.55 us
  transfers between devices with their start and end apart: 10, of which 8 were waited for; matrix products, arithmetic and copies ran while one was open for 17% of the time, Pallas kernels for 0%

commit v1 on v0

--- a/solution.py
+++ b/solution.py
@@ -40,16 +40,32 @@
 
 
 def shards(out_grad, x_in, b_in, c_in, dt_raw, dt_bias, a_log, d_skip, states, w_out, w_in):
+
+    def hold_series_all(block_in, row_axis):
+        piece_out = lax.axis_size(row_axis)
+        frame_out = lax.axis_index(row_axis)
+        w_next, before, newest = (piece_out, frame_out, block_in.shape[1])
+        f_next, x_next = (block_in, 1)
+        while x_next < w_next:
+            f_next = jnp.concatenate(
+                [
+                    f_next,
+                    lax.ppermute(
+                        f_next, row_axis, [(idx, (idx - x_next) % w_next) for idx in range(w_next)]
+                    ),
+                ],
+                axis=1,
+            )
+            x_next = 2 * x_next
+        return jnp.roll(f_next, before * newest, axis=1)
+
     tokens_here, inner_here = x_in.shape
     group_heads = dt_raw.shape[0]
     head_dim = inner_here // group_heads
     state_dim = b_in.shape[1]
     contract_last = (((1,), (1,)), ((), ()))
     head_sum = lax.dot_general(
-        lax.all_gather(out_grad, "head", axis=1, tiled=True),
-        w_out,
-        contract_last,
-        preferred_element_type=jnp.float32,
+        hold_series_all(out_grad, "head"), w_out, contract_last, preferred_element_type=jnp.float32
     )
     dy_heads = head_sum.astype(jnp.bfloat16).reshape(tokens_here, group_heads, head_dim)
     dy_wide = dy_heads.astype(jnp.float32)

time: 162 us -> 184 us (1.14)
  local copies, waits for them, and re-layouts: 21.4 us -> 30.9 us
  other arithmetic: 10.9 us -> 16.9 us
  starting transfers between devices: 9.59 us -> 14.4 us
  waiting for transfers between devices: 78.4 us -> 81.2 us
    ppermute x0 -> x2, waiting for transfers between devices: none -> 34.9 us  [hold_series_all(): lax.ppermute(f_next, row_axis, [(idx, (idx - x_next) % w_next) for idx in...]
    all_gather x1 -> x0, waiting for transfers between devices: 34.5 us -> none  [shards(): lax.all_gather(out_grad, 'head', axis=1, tiled=True)]
    ppermute x0 -> x2, starting transfers between devices: none -> 6.49 us  [hold_series_all(): lax.ppermute(f_next, row_axis, [(idx, (idx - x_next) % w_next) for idx in...]
    unnamed x60 -> x57, local copies, waits for them, and re-layouts: 2.2 us -> 6.76 us
    concatenate x0 -> x1, other arithmetic: none -> 2.14 us  [hold_series_all(): jnp.concatenate([f_next, lax.ppermute(f_next, row_axis, [(idx, (idx - x_n...]
    ppermute x2, waiting for transfers between devices: 0.15 us -> 2.24 us  [entering(): other_decay = lax.ppermute(decay, axis, pairs)]
    ppermute x2, starting transfers between devices: 3.51 us -> 1.49 us  [entering(): other_decay = lax.ppermute(decay, axis, pairs)]
  transfers between devices with their start and end apart: 10 -> 11, of which waited for: 8 -> 9; matrix products, arithmetic and copies ran while one was open for 17% -> 20% of each run, Pallas kernels for 0% -> 0%
where the time goes in v1:
time: 184 us; the launch traced here: 183 us
  waiting for transfers between devices  81.2 us (44%)
  local copies, waits for them, and re-layouts  30.9 us (17%)
  matrix products  25.5 us (14%)
  other arithmetic  16.9 us (9%)
  starting transfers between devices  14.4 us (8%)
  between operations  14.3 us (8%)
    ppermute x2, waiting for transfers between devices, hold_series_all(): lax.ppermute(f_next, row_axis, [(idx, (idx - x_next) % w_next) for idx in...  34.9 us
    reduce_scatter x1, waiting for transfers between devices, shards(): lax.psum_scatter(both.reshape(-1, tokens_here), 'head', scatter_dimension...  28.7 us
    ppermute x3, waiting for transfers between devices, entering(): lax.ppermute(state.astype(jnp.bfloat16), axis, pairs).astype(jnp.float32)  10.7 us
    dot_general x1, matrix products, shards(): lax.dot_general(hold_series_all(out_grad, 'head'), w_out, contract_last,...  7.1 us
    unnamed x57, local copies, waits for them, and re-layouts  6.76 us
    ppermute x2, starting transfers between devices, hold_series_all(): lax.ppermute(f_next, row_axis, [(idx, (idx - x_next) % w_next) for idx in...  6.49 us
    dot_general x1, matrix products, shards(): lax.dot_general(w_in, x_grad, contract_last, preferred_element_type=jnp.f...  5.81 us
    ppermute x3, waiting for transfers between devices, summed(): value = value + lax.ppermute(value, axis, partners(count, distance))  4.66 us
  transfers between devices with their start and end apart: 11, of which 9 were waited for; matrix products, arithmetic and copies ran while one was open for 20% of the time, Pallas kernels for 0%

profile of v1, /device:TPU:0, one launch (start us, length us, event | category | flops | bytes accessed | tf_op | source)
XLA Modules:
  0.0 183.2 jit_solution(11411019901324702024)
XLA Ops:
  7.2 5.1 %collective-permute-start = (bf16[256,1024]{1,0:T(8,128)(2,1)}, bf16[256,1024]{1,0:T(8,128)(2,1)S(1)}, u32[]{:S(2)}, u32[]{:S(2)}) collective-permute-start(bf16[256,1024]{1,0:T(8,128)(2,1)} %param.13), channel_id=1, source_target_pairs={{0,3},{1,0},{2,1},{3,2},{4,7},{5,4},{6,5},{7,6},{8,11},{9,8},{10,9... | collective-permute-start | bytes 1572872 | tf_op jit(solution)/shard_map/ppermute | solution.py:53
  13.0 0.8 copy.92
  16.7 1.5 fusion.41
  18.2 5.6 %collective-permute-done = bf16[256,1024]{1,0:T(8,128)(2,1)S(1)} collective-permute-done((bf16[256,1024]{1,0:T(8,128)(2,1)}, bf16[256,1024]{1,0:T(8,128)(2,1)S(1)}, u32[]{:S(2)}, u32[]{:S(2)}) %collective-permute-start) | collective-permute-done | bytes 524320 | tf_op jit(solution)/shard_map/ppermute | solution.py:53
  23.9 2.1 %pad_maximum_fusion.1 = bf16[256,2048]{1,0:T(8,128)(2,1)} fusion(bf16[256,1024]{1,0:T(8,128)(2,1)S(1)} %collective-permute-done, bf16[256,1024]{1,0:T(8,128)(2,1)} %param.13), kind=kLoop, calls=%fused_computation.40 | loop fusion | flops 2097152 | bytes 2097152 | tf_op jit(solution)/shard_map/concatenate | solution.py:50
  26.0 1.4 collective-permute-start.1
  27.5 1.3 copy.103
  28.8 1.2 copy.102
  30.1 1.6 copy.93
  31.7 1.6 copy.99
  33.9 0.9 constant_dynamic-update-slice_fusion.5
  34.8 0.9 fusion.59
  35.7 1.6 copy.114
  37.3 1.3 fusion.52
  38.5 1.5 collective-permute-start.5
  40.0 2.2 %collective-permute-done.5 = f32[16]{0:T(128)} collective-permute-done((f32[16]{0:T(128)}, f32[16]{0:T(128)}, u32[]{:S(2)}, u32[]{:S(2)}) %collective-permute-start.5) | collective-permute-done | bytes 96 | tf_op jit(solution)/shard_map/ppermute | solution.py:18
  42.2 1.3 broadcast_select_fusion
  43.5 0.9 constant_dynamic-update-slice_fusion.4
  44.4 29.3 %collective-permute-done.1 = bf16[256,2048]{1,0:T(8,128)(2,1)S(1)} collective-permute-done((bf16[256,2048]{1,0:T(8,128)(2,1)}, bf16[256,2048]{1,0:T(8,128)(2,1)S(1)}, u32[]{:S(2)}, u32[]{:S(2)}) %collective-permute-start.1) | collective-permute-done | bytes 1048608 | tf_op jit(solution)/shard_map/ppermute | solution.py:53
  73.6 1.1 constant_dynamic-update-slice_fusion.3
  74.7 0.9 constant_dynamic-update-slice_fusion.2
  75.5 0.9 constant_dynamic-update-slice_fusion.1
  76.4 1.0 constant_dynamic-update-slice_fusion
  77.5 7.1 %fusion.21 = (f32[1024]{0:T(1024)}, bf16[256,1024]{1,0:T(8,128)(2,1)S(1)}, bf16[256,1024]{1,0:T(8,128)(2,1)S(1)}) fusion(bf16[256,1024]{1,0:T(8,128)(2,1)S(1)} %copy-done.8, f32[256,1024]{1,0:T(8,128)S(1)} %copy-done.5, bf16[1024,4096]{1,0:T(8,128)(2,1)} %param.22, bf16[256,8192]{1,0:T(8,128)(2,1)} %constant_dynamic-update-slice_fusion, s32[]{:T(128)S(6)} %select_n.87), kind=kOutput, calls=%fused_computation.36 | convolution fusion | flops 2149317632 | bytes 13111300 | tf_op jit(solution)/shard_map/dot_general | solution.py:67
  85.4 4.1 %fusion.1 = (f32[16,256]{1,0:T(8,128)}, f32[16,256]{1,0:T(8,128)}, bf16[256,256]{1,0:T(8,128)(2,1)S(1)}) fusion(f32[16,256]{1,0:T(8,128)} %copy-done.12, f32[256,256]{1,0:T(8,128)S(1)} %copy-done.10, pred[256,256]{1,0:T(8,128)(4,1)} %iota_compare_fusion, bf16[256,16,64]{0,2,1:T(8,128)(2,1)S(1)} %bitcast.111, f32[256,16,64]{0,2,1:T(8,128)S(1)} %bitcast.117, ...), kind=kOutput, calls=%fused_computation.7 | convolution fusion | flops 146202624 | bytes 2097152 | tf_op jit(solution)/shard_map/ihp,jhp->hij/dot_general | solution.py:85
  89.5 0.9 fusion.54
  90.4 1.6 collective-permute-start.4
  92.0 2.3 %fusion.11 = f32[256,16,64]{0,2,1:T(8,128)} fusion(bf16[256,16,64]{0,2,1:T(8,128)(2,1)S(1)} %bitcast.112, f32[16,256]{1,0:T(8,128)S(1)} %copy-done.13, f32[256,256]{1,0:T(8,128)S(1)} %copy-done.11, pred[256,256]{1,0:T(8,128)(4,1)S(1)} %copy-done.14), kind=kOutput, calls=%fused_computation.21 | convolution fusion | flops 139460608 | bytes 1916928 | tf_op jit(solution)/shard_map/hij,ihp->jhp/dot_general | solution.py:87
  94.2 4.9 %collective-permute-done.4 = bf16[16,64,128]{2,1,0:T(8,128)(2,1)S(1)} collective-permute-done((bf16[16,64,128]{2,1,0:T(8,128)(2,1)S(1)}, bf16[16,64,128]{2,1,0:T(8,128)(2,1)S(1)}, u32[]{:S(2)}, u32[]{:S(2)}) %collective-permute-start.4) | collective-permute-done | bytes 262176 | tf_op jit(solution)/shard_map/ppermute | solution.py:19
  99.1 1.0 fusion.29
  100.2 1.6 collective-permute-start.6
  102.3 5.8 %collective-permute-done.6 = bf16[16,64,128]{2,1,0:T(8,128)(2,1)S(1)} collective-permute-done((bf16[16,64,128]{2,1,0:T(8,128)(2,1)S(1)}, bf16[16,64,128]{2,1,0:T(8,128)(2,1)S(1)}, u32[]{:S(2)}, u32[]{:S(2)}) %collective-permute-start.6) | collective-permute-done | bytes 262176 | tf_op jit(solution)/shard_map/ppermute | solution.py:19
  108.8 0.9 copy.105
  109.7 2.7 %multiply_reduce_fusion.1 = (f32[256,16]{0,1:T(8,128)}, f32[256,16]{0,1:T(8,128)}, bf16[256,16,64]{0,2,1:T(8,128)(2,1)S(1)}) fusion(f32[256,1024]{0,1:T(8,128)S(1)} %copy.102, f32[256,16,64]{0,2,1:T(8,128)} %fusion.11, f32[256,16]{0,1:T(8,128)} %copy.114, bf16[256,1024]{0,1:T(8,128)(2,1)S(1)} %copy.94, f32[16]{0:T(128)} %param.20, f32[256,16]{0,1:T(8,128)} %copy.99, ...), kind=kOutput, calls=%fused_computation.42 | convolution fusion | flops 71950336 | bytes 4079811 | tf_op jit(solution)/shard_map/jn,hpn->jhp/dot_general | solution.py:103
  112.4 5.8 %fusion = bf16[4096,256]{0,1:T(8,128)(2,1)S(1)} fusion(bf16[256,1024]{0,1:T(8,128)(2,1)S(1)} %bitcast.132, bf16[4096,1024]{1,0:T(8,128)(2,1)} %param.23), kind=kOutput, calls=%fused_computation.1 | convolution fusion | flops 2148532224 | bytes 11010048 | tf_op jit(solution)/shard_map/dot_general | solution.py:134
  118.2 2.8 %reshape.138 = bf16[4,1024,256]{1,0,2:T(4,128)(2,1)} reshape(bf16[4096,256]{0,1:T(8,128)(2,1)S(1)} %fusion) | data formatting | bytes 4194304 | tf_op jit(solution)/shard_map/reshape | solution.py:140
  121.0 2.8 %pad_maximum_fusion = bf16[4,1088,256]{1,0,2:T(4,128)(2,1)S(1)} fusion(bf16[4,64,256]{1,0,2:T(4,128)(2,1)} %copy.105, bf16[4,1024,256]{1,0,2:T(4,128)(2,1)} %reshape.138), kind=kLoop, calls=%fused_computation.9 | loop fusion | flops 4456448 | bytes 4456448 | tf_op jit(solution)/shard_map/concatenate | solution.py:138
  123.8 3.6 %copy.106 = bf16[4,1088,256]{2,1,0:T(8,128)(2,1)} copy(bf16[4,1088,256]{1,0,2:T(4,128)(2,1)S(1)} %pad_maximum_fusion) | data formatting | bytes 4456448 | tf_op jit(solution)/shard_map/concatenate | solution.py:138
  127.4 1.2 fusion.15
  132.2 1.5 multiply_reduce_fusion.2
  135.4 1.1 collective-permute-done.7
  136.6 1.5 collective-permute-start.8
  138.1 2.1 %collective-permute-done.8 = f32[3,16]{1,0:T(4,128)S(1)} collective-permute-done((f32[3,16]{1,0:T(4,128)S(1)}, f32[3,16]{1,0:T(4,128)S(1)}, u32[]{:S(2)}, u32[]{:S(2)}) %collective-permute-start.8) | collective-permute-done | bytes 224 | tf_op jit(solution)/shard_map/ppermute | solution.py:37
  140.2 1.6 collective-permute-start.9
  142.5 1.4 collective-permute-done.9
  144.5 28.7 %reduce-scatter.2.cloned.1.call-done = bf16[1088,256]{1,0:T(8,128)(2,1)} async-done(((bf16[4352,256]{1,0:T(8,128)(2,1)}), bf16[1088,256]{1,0:T(8,128)(2,1)}) %reduce-scatter.2.cloned.1.call-update) | async-done | bytes 557072 | tf_op jit(solution)/shard_map/reduce_scatter | solution.py:145
  173.1 1.9 %slice.49 = bf16[1024,256]{1,0:T(8,128)(2,1)} slice(bf16[1088,256]{1,0:T(8,128)(2,1)} %reduce-scatter.2.cloned.1.call-done), slice={[0:1024], [0:256]} | slice | bytes 1048576 | tf_op jit(solution)/shard_map/slice | solution.py:148
  175.0 1.4 slice.50
  (104 shorter events, 12.9 us)
Async XLA Ops:
  7.2 27.6 %copy-start = (bf16[256,128]{1,0:T(8,128)(2,1)S(1)}, bf16[256,128]{1,0:T(8,128)(2,1)}, u32[]{:S(2)}) copy-start(bf16[256,128]{1,0:T(8,128)(2,1)} %param.15) | copy-start | bytes 196612
  7.2 166.0 %reduce-scatter.2.cloned.1.call-start = ((), (), s32[]{:S(2)}) async-start(), calls=%async_computation.1 | async-start | bytes 2785280 | tf_op jit(solution)/shard_map/reduce_scatter | solution.py:145
  7.2 16.6 %collective-permute-start = (bf16[256,1024]{1,0:T(8,128)(2,1)}, bf16[256,1024]{1,0:T(8,128)(2,1)S(1)}, u32[]{:S(2)}, u32[]{:S(2)}) collective-permute-start(bf16[256,1024]{1,0:T(8,128)(2,1)} %param.13), channel_id=1, source_target_pairs={{0,3},{1,0},{2,1},{3,2},{4,7},{5,4},{6,5},{7,6},{8,11},{9,8},{10,9... | collective-permute-start | bytes 1572872 | tf_op jit(solution)/shard_map/ppermute | solution.py:53
  13.0 1.6 copy-start.23
  15.5 0.6 copy-start.12
  15.5 18.4 %copy-start.1 = (bf16[256,1024]{1,0:T(8,128)(2,1)S(1)}, bf16[256,1024]{1,0:T(8,128)(2,1)}, u32[]{:S(2)}) copy-start(bf16[256,1024]{1,0:T(8,128)(2,1)} %param.13) | copy-start | bytes 1572868
  16.2 21.1 %collective-permute-start.3 = (f32[16]{0:T(128)}, f32[16]{0:T(128)}, u32[]{:S(2)}, u32[]{:S(2)}) collective-permute-start(f32[16]{0:T(128)} %fusion.51), channel_id=1, source_target_pairs={{0,4},{4,0},{8,12},{12,8},{16,20},{20,16},{24,28},{28,24},{1,5},{5... | collective-permute-start | bytes 200 | tf_op jit(solution)/shard_map/ppermute | solution.py:18
  16.2 0.6 copy-start.21
  18.2 16.6 %copy-start.7 = (bf16[256,128]{1,0:T(8,128)(2,1)S(1)}, bf16[256,128]{1,0:T(8,128)(2,1)}, u32[]{:S(2)}) copy-start(bf16[256,128]{1,0:T(8,128)(2,1)} %param.16) | copy-start | bytes 196612
  26.0 47.6 %collective-permute-start.1 = (bf16[256,2048]{1,0:T(8,128)(2,1)}, bf16[256,2048]{1,0:T(8,128)(2,1)S(1)}, u32[]{:S(2)}, u32[]{:S(2)}) collective-permute-start(bf16[256,2048]{1,0:T(8,128)(2,1)} %pad_maximum_fusion.1), channel_id=1, source_target_pairs={{0,2},{1,3},{2,0},{3,1},{4,6},{5,7},{6,4},{7,5},{8,10},{9,11},{10,... | collective-permute-start | bytes 3145736 | tf_op jit(solution)/shard_map/ppermute | solution.py:53
  38.5 3.7 %collective-permute-start.5 = (f32[16]{0:T(128)}, f32[16]{0:T(128)}, u32[]{:S(2)}, u32[]{:S(2)}) collective-permute-start(f32[16]{0:T(128)} %fusion.52), channel_id=1, source_target_pairs={{0,8},{4,12},{8,0},{12,4},{16,24},{20,28},{24,16},{28,20},{1,9},{5... | collective-permute-start | bytes 200 | tf_op jit(solution)/shard_map/ppermute | solution.py:18
  40.0 37.5 %copy-start.5 = (f32[256,1024]{1,0:T(8,128)S(1)}, f32[256,1024]{1,0:T(8,128)}, u32[]{:S(2)}) copy-start(f32[256,1024]{1,0:T(8,128)} %copy.103) | copy-start | bytes 3145732
  40.0 37.5 %copy-start.8 = (bf16[256,1024]{1,0:T(8,128)(2,1)S(1)}, bf16[256,1024]{1,0:T(8,128)(2,1)}, u32[]{:S(2)}) copy-start(bf16[256,1024]{1,0:T(8,128)(2,1)} %param.14) | copy-start | bytes 1572868
  77.5 7.9 %copy-start.10 = (f32[256,256]{1,0:T(8,128)S(1)}, f32[256,256]{1,0:T(8,128)}, u32[]{:S(2)}) copy-start(f32[256,256]{1,0:T(8,128)} %fusion.59) | copy-start | bytes 786436
  85.0 24.7 %copy-start.2 = (bf16[256,1024]{0,1:T(8,128)(2,1)}, bf16[256,1024]{0,1:T(8,128)(2,1)S(1)}, u32[]{:S(2)}) copy-start(bf16[256,1024]{0,1:T(8,128)(2,1)S(1)} %copy.94) | copy-start | bytes 1572868
  85.3 4.2 %collective-permute-start.2 = (bf16[16,64,128]{2,1,0:T(8,128)(2,1)S(1)}, bf16[16,64,128]{2,1,0:T(8,128)(2,1)S(1)}, u32[]{:S(2)}, u32[]{:S(2)}) collective-permute-start(bf16[16,64,128]{2,1,0:T(8,128)(2,1)S(1)} %get-tuple-element.48), channel_id=1, source_target_pairs={{0,4},{4,0},{8,12},{12,8},{16,20},{20,16},{24,28},{28,24},{1,5},{5... | collective-permute-start | bytes 786440 | tf_op jit(solution)/shard_map/ppermute | solution.py:19
  85.4 6.6 %copy-start.11 = (f32[256,256]{1,0:T(8,128)S(1)}, f32[256,256]{1,0:T(8,128)}, u32[]{:S(2)}) copy-start(f32[256,256]{1,0:T(8,128)} %fusion.59) | copy-start | bytes 786436
  85.4 6.6 %copy-start.13 = (f32[16,256]{1,0:T(8,128)S(1)}, f32[16,256]{1,0:T(8,128)}, u32[]{:S(2)}) copy-start(f32[16,256]{1,0:T(8,128)} %copy-done.12) | copy-start | bytes 49156
  85.4 6.6 %copy-start.14 = (pred[256,256]{1,0:T(8,128)(4,1)S(1)}, pred[256,256]{1,0:T(8,128)(4,1)}, u32[]{:S(2)}) copy-start(pred[256,256]{1,0:T(8,128)(4,1)} %iota_compare_fusion) | copy-start | bytes 196612
  90.3 11.4 %copy-start.4 = (bf16[1,1024,128]{2,1,0:T(8,128)(2,1)S(1)}, bf16[1,1024,128]{2,1,0:T(8,128)(2,1)}, u32[]{:S(2)}) copy-start(bf16[1,1024,128]{2,1,0:T(8,128)(2,1)} %param.21) | copy-start | bytes 786436
  90.4 17.7 %copy-start.16 = (f32[256,16]{0,1:T(8,128)S(1)}, f32[256,16]{0,1:T(8,128)}, u32[]{:S(2)}) copy-start(f32[256,16]{0,1:T(8,128)} %copy.99) | copy-start | bytes 49156
  90.4 17.7 %copy-start.19 = (f32[16]{0:T(128)S(1)}, f32[16]{0:T(128)}, u32[]{:S(2)}) copy-start(f32[16]{0:T(128)} %get-tuple-element.35) | copy-start | bytes 196
  90.4 17.7 %copy-start.20 = (f32[16]{0:T(128)S(1)}, f32[16]{0:T(128)}, u32[]{:S(2)}) copy-start(f32[16]{0:T(128)} %get-tuple-element.36) | copy-start | bytes 196
  90.4 8.7 %collective-permute-start.4 = (bf16[16,64,128]{2,1,0:T(8,128)(2,1)S(1)}, bf16[16,64,128]{2,1,0:T(8,128)(2,1)S(1)}, u32[]{:S(2)}, u32[]{:S(2)}) collective-permute-start(bf16[16,64,128]{2,1,0:T(8,128)(2,1)S(1)} %fusion.54), channel_id=1, source_target_pairs={{0,8},{4,12},{8,0},{12,4},{16,24},{20,28},{24,16},{28,20},{1,9},{5... | collective-permute-start | bytes 786440 | tf_op jit(solution)/shard_map/ppermute | solution.py:19
  94.2 15.4 %copy-start.15 = (f32[256,16]{0,1:T(8,128)S(1)}, f32[256,16]{0,1:T(8,128)}, u32[]{:S(2)}) copy-start(f32[256,16]{0,1:T(8,128)} %copy.93) | copy-start | bytes 49156
  99.1 13.2 %copy-start.6 = (bf16[16,64,128]{2,1,0:T(8,128)(2,1)}, bf16[16,64,128]{2,1,0:T(8,128)(2,1)S(1)}, u32[]{:S(2)}) copy-start(bf16[16,64,128]{2,1,0:T(8,128)(2,1)S(1)} %collective-permute-done.4) | copy-start | bytes 786436
  100.2 7.9 %collective-permute-start.6 = (bf16[16,64,128]{2,1,0:T(8,128)(2,1)S(1)}, bf16[16,64,128]{2,1,0:T(8,128)(2,1)S(1)}, u32[]{:S(2)}, u32[]{:S(2)}) collective-permute-start(bf16[16,64,128]{2,1,0:T(8,128)(2,1)S(1)} %fusion.29), channel_id=1, source_target_pairs={{0,16},{4,20},{8,24},{12,28},{16,0},{20,4},{24,8},{28,12},{1,17},{... | collective-permute-start | bytes 786440 | tf_op jit(solution)/shard_map/ppermute | solution.py:19
  108.1 0.7 copy-start.9
  123.8 3.6 %copy-start.3 = (bf16[256,1024]{0,1:T(8,128)(2,1)S(1)}, bf16[256,1024]{0,1:T(8,128)(2,1)}, u32[]{:S(2)}) copy-start(bf16[256,1024]{0,1:T(8,128)(2,1)} %copy-done.2) | copy-start | bytes 1572868
  123.8 5.8 %copy-start.17 = (f32[16,256]{1,0:T(8,128)S(1)}, f32[16,256]{1,0:T(8,128)}, u32[]{:S(2)}) copy-start(f32[16,256]{1,0:T(8,128)} %get-tuple-element.28) | copy-start | bytes 49156
  127.4 6.4 %copy-start.18 = (f32[16]{0:T(128)S(1)}, f32[16]{0:T(128)}, u32[]{:S(2)}) copy-start(f32[16]{0:T(128)} %param.18) | copy-start | bytes 196
  127.4 6.4 %copy-start.22 = (f32[16]{0:T(128)S(1)}, f32[16]{0:T(128)}, u32[]{:S(2)}) copy-start(f32[16]{0:T(128)} %copy-done.21) | copy-start | bytes 196
  127.4 7.8 %copy-start.24 = (f32[16]{0:T(128)S(1)}, f32[16]{0:T(128)}, u32[]{:S(2)}) copy-start(f32[16]{0:T(128)} %copy-done.23) | copy-start | bytes 196
  135.3 1.2 collective-permute-start.7
  136.6 3.7 %collective-permute-start.8 = (f32[3,16]{1,0:T(4,128)S(1)}, f32[3,16]{1,0:T(4,128)S(1)}, u32[]{:S(2)}, u32[]{:S(2)}) collective-permute-start(f32[3,16]{1,0:T(4,128)S(1)} %fusion.53), channel_id=1, source_target_pairs={{0,8},{4,12},{8,0},{12,4},{16,24},{20,28},{24,16},{28,20},{1,9},{5... | collective-permute-start | bytes 584 | tf_op jit(solution)/shard_map/ppermute | solution.py:37
  140.2 3.7 %collective-permute-start.9 = (f32[3,16]{1,0:T(4,128)S(1)}, f32[3,16]{1,0:T(4,128)S(1)}, u32[]{:S(2)}, u32[]{:S(2)}) collective-permute-start(f32[3,16]{1,0:T(4,128)S(1)} %fusion.74), channel_id=1, source_target_pairs={{0,16},{4,20},{8,24},{12,28},{16,0},{20,4},{24,8},{28,12},{1,17},{... | collective-permute-start | bytes 584 | tf_op jit(solution)/shard_map/ppermute | solution.py:37
Sparse Core Ops, SparseCore 0:
  127.5 45.5 reduce-scatter.1
